TPU v7x, 32 devices: a whole 2x2x4 slice. The times are simulated.
32 devices in a mesh: tile: 8 (over y, x, core), col: 4 (over z).
Axes of the slice: x: 2, y: 2, z: 4, core: 2. Of those that a mesh axis runs over, the one named last changes fastest.
Arguments:
- impedance: bfloat16 [2, 16384, 16384], P(None, 'tile', 'col'), may hold values from -0.0234375 to 0.0234375
- mobility: bfloat16 [256, 64, 128], P('tile'), may hold values from -0.5 to 0.5
- force: bfloat16 [512, 256, 128], P('col', 'tile'), may hold values from -6 to 6
- patch_map: int32 [16384], replicated, may hold values from 0 to 16383, each once
- ownership: int32 [256], P('tile'), may hold values from 0 to 255, each once
Outputs:
- velocity: bfloat16 [512, 256, 128], P('col', 'tile')
- pressure: bfloat16 [512, 2, 16384], P('col', None, 'tile')
Inputs may be any that keep to these rules, and one draw needn't show every extreme that they name: `patch_map`: each patch appears exactly once. `ownership`: each panel appears exactly once.
All inputs are finite; a program needn't handle non-finite values.
Results may differ from a plain program's by a relative error of at most 0.018.
Values may be sent and summed in bfloat16 or wider, within the bound.
A program may use at most 128 MiB of HBM per device.

v0:
```python
import jax
import jax.numpy as jnp
from jax import lax
from jax.sharding import PartitionSpec as P

ITERS = 2


def per_device(impedance, mobility, force, patch_map, ownership):
    imp_re = impedance[0]
    imp_im = impedance[1]
    panel_width = mobility.shape[1]
    slot_count = mobility.shape[0]
    patch_count = patch_map.shape[0]
    loads_dev = force.shape[0]
    col_tiles = lax.axis_size("col")
    col_width = patch_count // col_tiles
    row_width = imp_re.shape[0]
    slot_flat = patch_map.reshape(-1, panel_width)[ownership].reshape(slot_count * panel_width)
    mob_re_t = jnp.transpose(mobility[:, :, :panel_width], (0, 2, 1))
    mob_im_t = jnp.transpose(mobility[:, :, panel_width:], (0, 2, 1))
    upper_rows = jnp.concatenate([mob_re_t, mob_im_t], 2)
    lower_rows = jnp.concatenate([-mob_im_t, mob_re_t], 2)
    real_form = jnp.concatenate([upper_rows, lower_rows], 1)

    def panel_response(drive):
        return jnp.einsum(
            "lsk,skj->lsj", drive, real_form, preferred_element_type=jnp.float32
        ).astype(jnp.bfloat16)

    velocity = panel_response(force)
    pressure = jnp.zeros((loads_dev, 2, row_width), jnp.bfloat16)
    for iteration in range(ITERS):
        values = (
            velocity.reshape(loads_dev, slot_count, 2, panel_width)
            .transpose(0, 2, 1, 3)
            .reshape(loads_dev, 2 * slot_count * panel_width)
        )
        base_pos = slot_flat // col_width * (2 * col_width) + slot_flat % col_width
        flat_index = jnp.concatenate([base_pos, base_pos + col_width])
        placed = jnp.zeros((loads_dev, 2 * patch_count), jnp.bfloat16).at[:, flat_index].set(values)
        placed = placed.reshape(loads_dev, col_tiles, 2, col_width)
        shares = lax.psum_scatter(
            placed.astype(jnp.float32).astype(jnp.bfloat16), "tile", scatter_dimension=3, tiled=True
        )
        moved = lax.all_to_all(shares, "col", split_axis=1, concat_axis=0, tiled=True)
        full_cols = lax.all_gather(moved, "tile", axis=3, tiled=True)
        columns = full_cols.reshape(full_cols.shape[0], 2 * col_width)
        vel_re = columns[:, :col_width]
        vel_im = columns[:, col_width:]
        contract = (((1,), (1,)), ((), ()))

        def dot_rows(left, right):
            return lax.dot_general(left, right, contract, preferred_element_type=jnp.float32)

        real_part = dot_rows(vel_re, imp_re) - dot_rows(vel_im, imp_im)
        imag_part = dot_rows(vel_re, imp_im) + dot_rows(vel_im, imp_re)
        summed = lax.psum_scatter(
            jnp.concatenate([real_part, imag_part], 1).astype(jnp.bfloat16),
            "col",
            scatter_dimension=0,
            tiled=True,
        )
        pressure = summed.reshape(loads_dev, 2, row_width)
        gathered = lax.all_gather(pressure, "tile", axis=2, tiled=True)
        picked = (
            gathered[:, :, slot_flat]
            .reshape(loads_dev, 2, slot_count, panel_width)
            .transpose(0, 2, 1, 3)
            .reshape(loads_dev, slot_count, 2 * panel_width)
        )
        drive = (force.astype(jnp.float32) - picked.astype(jnp.float32)).astype(jnp.bfloat16)
        velocity = panel_response(drive)
    return (velocity, pressure)


def solution(mesh):
    return jax.shard_map(
        per_device,
        mesh=mesh,
        in_specs=(
            P(None, "tile", "col"),
            P("tile", None, None),
            P("col", "tile", None),
            P(),
            P("tile"),
        ),
        out_specs=(P("col", "tile", None), P("col", None, "tile")),
        check_vma=False,
    )
```

profile of v0, /device:TPU:0, one launch (start us, length us, event | category | flops | bytes accessed | tf_op | source)
XLA Modules:
  0.0 846.8 jit_solution(14066625259313548850)
XLA Ops:
  7.2 1.3 fusion.61
  8.6 2.4 slice_bitcast_fusion
  11.0 0.7 compare_select_fusion.2
  11.6 0.9 reshape.153
  12.6 0.6 gather_fusion
  13.1 0.1 reshape.154
  13.2 1.0 copy.47
  14.2 1.9 convolution_convert_fusion.2
  16.2 0.1 copy.49
  16.3 15.8 %scatter_custom_fusion = bf16[128,32768]{0,1:T(8,128)(2,1)} fusion(s32[4096]{0:T(1024)S(1)} %bitcast.108, bf16[4096,128]{1,0:T(8,128)(2,1)S(1)} %bitcast.101, bf16[]{:T(256)} %constant.36.clone.1), kind=kCustom, calls=%fused_computation.37 | custom fusion | bytes 8388610 | tf_op jit(solution)/shard_map/scatter | solution.py:41
  32.1 11.6 %copy.50 = bf16[128,4,2,4096]{3,0,2,1:T(8,128)(2,1)} copy(bf16[128,4,2,4096]{0,3,2,1:T(8,128)(2,1)} %bitcast.88) | data formatting | bytes 16777216 | tf_op jit(solution)/shard_map/reshape | solution.py:42
  43.8 74.1 %reduce-scatter.5.cloned.1.call-done = bf16[128,4,2,512]{3,0,2,1:T(8,128)(2,1)} async-done(((bf16[128,4,2,4096]{3,0,2,1:T(8,128)(2,1)}), bf16[128,4,2,512]{3,0,2,1:T(8,128)(2,1)}) %reduce-scatter.5.cloned.1.call-update) | async-done | bytes 1048592 | tf_op jit(solution)/shard_map/reduce_scatter | solution.py:43
  117.9 30.1 %all_to_all.36 = bf16[128,4,2,512]{3,0,2,1:T(8,128)(2,1)S(1)} all-to-all(bf16[128,4,2,512]{3,0,2,1:T(8,128)(2,1)} %reduce-scatter.5.cloned.1.call-done), channel_id=1, replica_groups=mesh['tile'=8,'col'=4] {'col'}, dimensions={1} | all-to-all | bytes 2097152 | tf_op jit(solution)/shard_map/all_to_all | solution.py:46
  148.0 1.1 copy.51
  149.1 0.3 reduce-scatter.7.cloned.1.call-start
  149.4 53.9 %all-gather.5.cloned.1.call-done = bf16[512,1,2,4096]{3,0,2,1:T(8,128)(2,1)} async-done(((bf16[512,1,2,512]{3,0,2,1:T(8,128)(2,1)}), bf16[512,1,2,4096]{3,0,2,1:T(8,128)(2,1)}) %all-gather.5.cloned.1.call-update) | async-done | bytes 8388624 | tf_op jit(solution)/shard_map/all_gather | solution.py:47
  203.3 12.0 %copy.52 = bf16[512,1,2,4096]{0,3,2,1:T(8,128)(2,1)} copy(bf16[512,1,2,4096]{3,0,2,1:T(8,128)(2,1)} %all-gather.5.cloned.1.call-done) | data formatting | bytes 16777216 | tf_op jit(solution)/shard_map/all_gather | solution.py:47
  215.3 17.2 %fusion.4 = f32[512,2048]{1,0:T(8,128)} fusion(bf16[2,2048,4096]{2,1,0:T(8,128)(2,1)} %param.5, bf16[512,8192]{0,1:T(8,128)(2,1)} %bitcast.89), kind=kOutput, calls=%fused_computation.9 | convolution fusion | flops 8589934592 | bytes 25165824 | tf_op jit(solution)/shard_map/dot_general | solution.py:54
  232.5 14.1 %fusion.6 = f32[512,2048]{1,0:T(8,128)} fusion(bf16[2,2048,4096]{2,1,0:T(8,128)(2,1)} %param.5, bf16[512,8192]{0,1:T(8,128)(2,1)S(1)} %bitcast.92), kind=kOutput, calls=%fused_computation.11 | convolution fusion | flops 8589934592 | bytes 25165824 | tf_op jit(solution)/shard_map/dot_general | solution.py:54
  246.6 14.7 %add_convert_fusion.1 = bf16[512,2048]{1,0:T(8,128)(2,1)S(1)} fusion(f32[512,2048]{1,0:T(8,128)} %fusion.4, bf16[2,2048,4096]{2,1,0:T(8,128)(2,1)} %param.5, bf16[512,8192]{0,1:T(8,128)(2,1)} %bitcast.90), kind=kOutput, calls=%fused_computation.33 | convolution fusion | flops 8592031744 | bytes 27262976 | tf_op jit(solution)/shard_map/dot_general | solution.py:54
  261.3 14.3 %subtract_convert_fusion.1 = bf16[512,2048]{1,0:T(8,128)(2,1)S(1)} fusion(f32[512,2048]{1,0:T(8,128)} %fusion.6, bf16[2,2048,4096]{2,1,0:T(8,128)(2,1)} %param.5, bf16[512,8192]{0,1:T(8,128)(2,1)} %bitcast.91), kind=kOutput, calls=%fused_computation.34 | convolution fusion | flops 8592031744 | bytes 27262976 | tf_op jit(solution)/shard_map/dot_general | solution.py:54
  275.6 2.2 pad_maximum_fusion
  277.9 76.9 %reduce-scatter.7.cloned.1.call-done = bf16[128,4096]{1,0:T(8,128)(2,1)} async-done(((bf16[512,4096]{1,0:T(8,128)(2,1)}), bf16[128,4096]{1,0:T(8,128)(2,1)}) %reduce-scatter.7.cloned.1.call-update) | async-done | bytes 1048592 | tf_op jit(solution)/shard_map/reduce_scatter | solution.py:58
  354.8 1.8 reshape.159
  356.7 3.1 copy.53
  359.8 0.1 reshape.160
  359.9 54.8 %all-gather.7.cloned.1.call-done = bf16[128,2,16384]{0,1,2:T(2,128)(2,1)} async-done(((bf16[128,2,2048]{0,1,2:T(2,128)(2,1)}), bf16[128,2,16384]{0,1,2:T(2,128)(2,1)}) %all-gather.7.cloned.1.call-update) | async-done | bytes 8388624 | tf_op jit(solution)/shard_map/all_gather | solution.py:65
  414.7 10.6 %gather_fusion.1 = bf16[2048,128,2]{1,2,0:T(2,128)(2,1)S(1)} fusion(bf16[128,2,16384]{0,1,2:T(2,128)(2,1)} %all-gather.7.cloned.1.call-done, s32[2048]{0:T(1024)S(1)} %broadcast_clamp_fusion), kind=kCustom, calls=%fused_computation.1 | custom fusion | bytes 2105344 | tf_op jit(solution)/shard_map/gather | solution.py:67
  425.3 0.8 convert_bitcast_fusion.1
  426.1 0.1 copy.54
  426.2 0.2 copy.55
  426.5 0.3 fusion.52
  426.8 0.4 copy-done.5
  427.2 0.2 copy-done.8
  427.4 0.2 copy-done.10
  427.6 0.7 convolution_convert_fusion.1
  428.3 0.1 copy.57
  428.3 15.8 %scatter_custom_fusion.1 = bf16[128,32768]{0,1:T(8,128)(2,1)} fusion(s32[4096]{0:T(1024)S(1)} %bitcast.109, bf16[4096,128]{1,0:T(8,128)(2,1)S(1)} %bitcast.102, bf16[]{:T(256)} %constant.36.clone.1), kind=kCustom, calls=%fused_computation.35 | custom fusion | bytes 8388610 | tf_op jit(solution)/shard_map/scatter | solution.py:41
  444.1 11.6 %copy.58 = bf16[128,4,2,4096]{3,0,2,1:T(8,128)(2,1)} copy(bf16[128,4,2,4096]{0,3,2,1:T(8,128)(2,1)} %bitcast.87) | data formatting | bytes 16777216 | tf_op jit(solution)/shard_map/reshape | solution.py:42
  455.8 71.4 %reduce-scatter.9.cloned.1.call-done = bf16[128,4,2,512]{3,0,2,1:T(8,128)(2,1)} async-done(((bf16[128,4,2,4096]{3,0,2,1:T(8,128)(2,1)}), bf16[128,4,2,512]{3,0,2,1:T(8,128)(2,1)}) %reduce-scatter.9.cloned.1.call-update) | async-done | bytes 1048592 | tf_op jit(solution)/shard_map/reduce_scatter | solution.py:43
  527.2 30.2 %all_to_all.37 = bf16[128,4,2,512]{3,0,2,1:T(8,128)(2,1)S(1)} all-to-all(bf16[128,4,2,512]{3,0,2,1:T(8,128)(2,1)} %reduce-scatter.9.cloned.1.call-done), channel_id=1, replica_groups=mesh['tile'=8,'col'=4] {'col'}, dimensions={1} | all-to-all | bytes 2097152 | tf_op jit(solution)/shard_map/all_to_all | solution.py:46
  557.4 1.1 copy.59
  558.5 0.0 reduce-scatter.11.cloned.1.call-start
  558.5 54.1 %all-gather.9.cloned.1.call-done = bf16[512,1,2,4096]{3,0,2,1:T(8,128)(2,1)} async-done(((bf16[512,1,2,512]{3,0,2,1:T(8,128)(2,1)}), bf16[512,1,2,4096]{3,0,2,1:T(8,128)(2,1)}) %all-gather.9.cloned.1.call-update) | async-done | bytes 8388624 | tf_op jit(solution)/shard_map/all_gather | solution.py:47
  612.6 12.2 %copy.60 = bf16[512,1,2,4096]{0,3,2,1:T(8,128)(2,1)} copy(bf16[512,1,2,4096]{3,0,2,1:T(8,128)(2,1)} %all-gather.9.cloned.1.call-done) | data formatting | bytes 16777216 | tf_op jit(solution)/shard_map/all_gather | solution.py:47
  624.9 17.2 %fusion = f32[512,2048]{1,0:T(8,128)} fusion(bf16[2,2048,4096]{2,1,0:T(8,128)(2,1)} %param.5, bf16[512,8192]{0,1:T(8,128)(2,1)} %bitcast.93), kind=kOutput, calls=%fused_computation.5 | convolution fusion | flops 8589934592 | bytes 25165824 | tf_op jit(solution)/shard_map/dot_general | solution.py:54
  642.1 14.1 %fusion.2 = f32[512,2048]{1,0:T(8,128)} fusion(bf16[2,2048,4096]{2,1,0:T(8,128)(2,1)} %param.5, bf16[512,8192]{0,1:T(8,128)(2,1)S(1)} %bitcast.96), kind=kOutput, calls=%fused_computation.7 | convolution fusion | flops 8589934592 | bytes 25165824 | tf_op jit(solution)/shard_map/dot_general | solution.py:54
  656.1 14.6 %add_convert_fusion = bf16[512,2048]{1,0:T(8,128)(2,1)S(1)} fusion(f32[512,2048]{1,0:T(8,128)} %fusion, bf16[2,2048,4096]{2,1,0:T(8,128)(2,1)} %param.5, bf16[512,8192]{0,1:T(8,128)(2,1)} %bitcast.94), kind=kOutput, calls=%fused_computation.31 | convolution fusion | flops 8592031744 | bytes 27262976 | tf_op jit(solution)/shard_map/dot_general | solution.py:54
  670.7 14.3 %subtract_convert_fusion = bf16[512,2048]{1,0:T(8,128)(2,1)S(1)} fusion(f32[512,2048]{1,0:T(8,128)} %fusion.2, bf16[2,2048,4096]{2,1,0:T(8,128)(2,1)} %param.5, bf16[512,8192]{0,1:T(8,128)(2,1)} %bitcast.95), kind=kOutput, calls=%fused_computation.32 | convolution fusion | flops 8592031744 | bytes 27262976 | tf_op jit(solution)/shard_map/dot_general | solution.py:54
  685.1 2.2 pad_maximum_fusion.1
  687.3 76.9 %reduce-scatter.11.cloned.1.call-done = bf16[128,4096]{1,0:T(8,128)(2,1)} async-done(((bf16[512,4096]{1,0:T(8,128)(2,1)}), bf16[128,4096]{1,0:T(8,128)(2,1)}) %reduce-scatter.11.cloned.1.call-update) | async-done | bytes 1048592 | tf_op jit(solution)/shard_map/reduce_scatter | solution.py:58
  764.2 2.1 reshape.165
  766.4 3.1 copy.61
  769.5 54.9 %all-gather.11.cloned.1.call-done = bf16[128,2,16384]{0,1,2:T(2,128)(2,1)} async-done(((bf16[128,2,2048]{0,1,2:T(2,128)(2,1)}), bf16[128,2,16384]{0,1,2:T(2,128)(2,1)}) %all-gather.11.cloned.1.call-update) | async-done | bytes 8388624 | tf_op jit(solution)/shard_map/all_gather | solution.py:65
  824.4 10.4 %gather_fusion.2 = bf16[2048,128,2]{1,2,0:T(2,128)(2,1)S(1)} fusion(bf16[128,2,16384]{0,1,2:T(2,128)(2,1)} %all-gather.11.cloned.1.call-done, s32[2048]{0:T(1024)S(1)} %broadcast_clamp_fusion), kind=kCustom, calls=%fused_computation.2 | custom fusion | bytes 2105344 | tf_op jit(solution)/shard_map/gather | solution.py:67
  834.8 0.8 convert_bitcast_fusion
  835.6 0.1 copy.62
  835.8 0.2 copy.63
  836.0 0.3 fusion.53
  836.4 0.4 copy-done.6
  836.8 0.2 copy-done.9
  836.9 0.2 copy-done.11
  837.1 0.7 fusion.54
  837.8 1.7 copy.65
  (37 shorter events, 0.5 us)
Async XLA Ops:
  7.2 6.1 copy-start.3
  7.2 110.7 %reduce-scatter.5.cloned.1.call-start = ((), (), s32[]{:S(2)}) async-start(), calls=%async_computation.6 | async-start | bytes 9437184 | tf_op jit(solution)/shard_map/reduce_scatter | solution.py:43
  8.6 7.6 copy-start.4
  11.0 5.3 copy-start.7
  43.7 159.6 %all-gather.5.cloned.1.call-start = ((), (), s32[]{:S(2)}) async-start(), calls=%async_computation.7 | async-start | bytes 9437184 | tf_op jit(solution)/shard_map/all_gather | solution.py:47
  149.1 205.7 %reduce-scatter.7.cloned.1.call-start = ((), (), s32[]{:S(2)}) async-start(), calls=%async_computation.8 | async-start | bytes 5242880 | tf_op jit(solution)/shard_map/reduce_scatter | solution.py:58
  215.3 17.2 %copy-start = (bf16[512,1,2,4096]{0,3,2,1:T(8,128)(2,1)S(1)}, bf16[512,1,2,4096]{0,3,2,1:T(8,128)(2,1)}, u32[]{:S(2)}) copy-start(bf16[512,1,2,4096]{0,3,2,1:T(8,128)(2,1)} %copy.52) | copy-start | bytes 25165828
  277.9 136.8 %all-gather.7.cloned.1.call-start = ((), (), s32[]{:S(2)}) async-start(), calls=%async_computation.9 | async-start | bytes 9437184 | tf_op jit(solution)/shard_map/all_gather | solution.py:65
  359.8 167.5 %reduce-scatter.9.cloned.1.call-start = ((), (), s32[]{:S(2)}) async-start(), calls=%async_computation.10 | async-start | bytes 9437184 | tf_op jit(solution)/shard_map/reduce_scatter | solution.py:43
  426.2 1.0 copy-start.5
  426.2 1.2 copy-start.8
  426.2 1.3 copy-start.10
  455.8 156.9 %all-gather.9.cloned.1.call-start = ((), (), s32[]{:S(2)}) async-start(), calls=%async_computation.11 | async-start | bytes 9437184 | tf_op jit(solution)/shard_map/all_gather | solution.py:47
  558.5 205.8 %reduce-scatter.11.cloned.1.call-start = ((), (), s32[]{:S(2)}) async-start(), calls=%async_computation.12 | async-start | bytes 5242880 | tf_op jit(solution)/shard_map/reduce_scatter | solution.py:58
  624.9 17.2 %copy-start.1 = (bf16[512,1,2,4096]{0,3,2,1:T(8,128)(2,1)S(1)}, bf16[512,1,2,4096]{0,3,2,1:T(8,128)(2,1)}, u32[]{:S(2)}) copy-start(bf16[512,1,2,4096]{0,3,2,1:T(8,128)(2,1)} %copy.60) | copy-start | bytes 25165828
  687.3 137.1 %all-gather.11.cloned.1.call-start = ((), (), s32[]{:S(2)}) async-start(), calls=%async_computation.13 | async-start | bytes 9437184 | tf_op jit(solution)/shard_map/all_gather | solution.py:65
  766.4 69.2 %copy-start.2 = (bf16[128,2,2048]{2,1,0:T(2,128)(2,1)}, bf16[128,2,2048]{2,1,0:T(2,128)(2,1)S(1)}, u32[]{:S(2)}) copy-start(bf16[128,2,2048]{2,1,0:T(2,128)(2,1)S(1)} %reshape.165) | copy-start | bytes 3145732
  835.7 1.0 copy-start.6
  835.8 1.2 copy-start.9
  835.8 1.3 copy-start.11
Sparse Core Ops, SparseCore 0:
  43.8 73.9 reduce-scatter.4
  149.2 53.9 all-gather.4
  278.0 76.7 reduce-scatter.6
  359.9 54.7 all-gather.6
  455.9 71.2 reduce-scatter.8
  558.6 53.9 all-gather.8
  687.4 76.7 reduce-scatter.10
  769.6 54.7 all-gather.10
where the time goes:
time: 855 us; the launch traced here: 847 us
  waiting for transfers between devices  517 us (60%)
  matrix products  124 us (15%)
  local copies, waits for them, and re-layouts  121 us (14%)
  blocking collectives  60.3 us (7%)
  between operations  15 us (2%)
  other arithmetic  8.68 us (1%)
    reduce_scatter x2, waiting for transfers between devices, per_device(): lax.psum_scatter(jnp.concatenate([real_part, imag_part], 1).astype(jnp.bf...  154 us
    reduce_scatter x2, waiting for transfers between devices, per_device(): lax.psum_scatter(placed.astype(jnp.float32).astype(jnp.bfloat16), 'tile',...  146 us
    dot_general x8, matrix products, dot_rows(): lax.dot_general(left, right, contract, preferred_element_type=jnp.float32)  121 us
    all_gather x2, waiting for transfers between devices, per_device(): gathered = lax.all_gather(pressure, 'tile', axis=2, tiled=True)  110 us
    all_gather x2, waiting for transfers between devices, per_device(): full_cols = lax.all_gather(moved, 'tile', axis=3, tiled=True)  108 us
    all_to_all x2, blocking collectives, per_device(): lax.all_to_all(shares, 'col', split_axis=1, concat_axis=0, tiled=True)  60.3 us
    scatter x2, local copies, waits for them, and re-layouts, per_device(): jnp.zeros((loads_dev, 2 * patch_count), jnp.bfloat16).at[:, flat_index]  31.5 us
    all_gather x2, local copies, waits for them, and re-layouts, per_device(): full_cols = lax.all_gather(moved, 'tile', axis=3, tiled=True)  24.2 us
  transfers between devices with their start and end apart: 8, of which 8 were waited for; matrix products, arithmetic and copies ran while one was open for 0% of the time, Pallas kernels for 0%

commit v1 on v0

--- a/solution.py
+++ b/solution.py
@@ -4,6 +4,18 @@
 from jax.sharding import PartitionSpec as P
 
 ITERS = 2
+
+
+def sent_to_each(shard, axis, split, join):
+    ways, here = (lax.axis_size(axis), lax.axis_index(axis))
+    width = shard.shape[split] // ways
+    turned = jnp.roll(shard, -here * width, axis=split)
+    got = [lax.slice_in_dim(turned, 0, width, axis=split)]
+    for far in range(1, ways):
+        sent = lax.slice_in_dim(turned, far * width, (far + 1) * width, axis=split)
+        got.append(lax.ppermute(sent, axis, [(d, (d + far) % ways) for d in range(ways)]))
+    line = jnp.concatenate(got[::-1], axis=join)
+    return jnp.roll(line, (here + 1) * got[0].shape[join], axis=join)
 
 
 def per_device(impedance, mobility, force, patch_map, ownership):
@@ -43,7 +55,7 @@
         shares = lax.psum_scatter(
             placed.astype(jnp.float32).astype(jnp.bfloat16), "tile", scatter_dimension=3, tiled=True
         )
-        moved = lax.all_to_all(shares, "col", split_axis=1, concat_axis=0, tiled=True)
+        moved = sent_to_each(shares, "col", 1, 0)
         full_cols = lax.all_gather(moved, "tile", axis=3, tiled=True)
         columns = full_cols.reshape(full_cols.shape[0], 2 * col_width)
         vel_re = columns[:, :col_width]

time: 855 us -> 802 us (0.938)
  blocking collectives: 60.3 us -> 0 us
  local copies, waits for them, and re-layouts: 121 us -> 72.5 us
  waiting for transfers between devices: 517 us -> 557 us
  starting transfers between devices: 0.54 us -> 11.2 us
    all_to_all x2 -> x0, blocking collectives: 60.3 us -> none  [per_device(): lax.all_to_all(shares, 'col', split_axis=1, concat_axis=0, tiled=True)]
    ppermute x0 -> x6, waiting for transfers between devices: none -> 31.7 us  [sent_to_each(): lax.ppermute(sent, axis, [(d, (d + far) % ways) for d in range(ways)])]
    all_gather x2 -> x0, local copies, waits for them, and re-layouts: 24.2 us -> none  [per_device(): full_cols = lax.all_gather(moved, 'tile', axis=3, tiled=True)]
    reshape x2 -> x0, local copies, waits for them, and re-layouts: 23.3 us -> none  [per_device(): placed = placed.reshape(loads_dev, col_tiles, 2, col_width)]
    ppermute x0 -> x6, starting transfers between devices: none -> 10.6 us  [sent_to_each(): lax.ppermute(sent, axis, [(d, (d + far) % ways) for d in range(ways)])]
  transfers between devices with their start and end apart: 8 -> 14, of which waited for: 8 -> 12; matrix products, arithmetic and copies ran while one was open for 0% -> 0% of each run, Pallas kernels for 0% -> 0%
where the time goes in v1:
time: 802 us; the launch traced here: 794 us
  waiting for transfers between devices  557 us (69%)
  matrix products  123 us (15%)
  local copies, waits for them, and re-layouts  72.5 us (9%)
  other arithmetic  16.4 us (2%)
  between operations  15 us (2%)
  starting transfers between devices  11.2 us (1%)
    reduce_scatter x2, waiting for transfers between devices, per_device(): lax.psum_scatter(jnp.concatenate([real_part, imag_part], 1).astype(jnp.bf...  154 us
    reduce_scatter x2, waiting for transfers between devices, per_device(): lax.psum_scatter(placed.astype(jnp.float32).astype(jnp.bfloat16), 'tile',...  146 us
    dot_general x8, matrix products, dot_rows(): lax.dot_general(left, right, contract, preferred_element_type=jnp.float32)  119 us
    all_gather x2, waiting for transfers between devices, per_device(): full_cols = lax.all_gather(moved, 'tile', axis=3, tiled=True)  116 us
    all_gather x2, waiting for transfers between devices, per_device(): gathered = lax.all_gather(pressure, 'tile', axis=2, tiled=True)  110 us
    ppermute x6, waiting for transfers between devices, sent_to_each(): lax.ppermute(sent, axis, [(d, (d + far) % ways) for d in range(ways)])  31.7 us
    scatter x2, local copies, waits for them, and re-layouts, per_device(): jnp.zeros((loads_dev, 2 * patch_count), jnp.bfloat16).at[:, flat_index]  31.6 us
    gather x2, local copies, waits for them, and re-layouts, per_device(): gathered[:, :, slot_flat].reshape(loads_dev, 2, slot_count, panel_width)  21 us
  transfers between devices with their start and end apart: 14, of which 12 were waited for; matrix products, arithmetic and copies ran while one was open for 0% of the time, Pallas kernels for 0%

profile of v1, /device:TPU:0, one launch (start us, length us, event | category | flops | bytes accessed | tf_op | source)
XLA Modules:
  0.0 794.4 jit_solution(9934938635551782630)
XLA Ops:
  7.2 1.3 fusion.77
  8.6 2.4 slice_bitcast_fusion
  11.0 0.7 compare_select_fusion.2
  11.6 0.9 reshape.153
  12.6 0.6 gather_fusion
  13.2 1.0 copy.28
  14.2 1.9 convolution_convert_fusion.2
  16.2 15.8 %scatter_custom_fusion = bf16[128,32768]{0,1:T(8,128)(2,1)} fusion(s32[4096]{0:T(1024)S(1)} %bitcast.88, bf16[4096,128]{1,0:T(8,128)(2,1)S(1)} %bitcast.81, bf16[]{:T(256)} %constant.73.clone.1), kind=kCustom, calls=%fused_computation.37 | custom fusion | bytes 8388610 | tf_op jit(solution)/shard_map/scatter | solution.py:53
  32.2 74.2 %reduce-scatter.5.cloned.1.call-done = bf16[128,4,2,512]{0,3,2,1:T(8,128)(2,1)} async-done(((bf16[128,4,2,4096]{0,3,2,1:T(8,128)(2,1)}), bf16[128,4,2,512]{0,3,2,1:T(8,128)(2,1)}) %reduce-scatter.5.cloned.1.call-update) | async-done | bytes 1048592 | tf_op jit(solution)/shard_map/reduce_scatter | solution.py:55
  106.4 1.6 fusion.70
  108.0 0.9 fusion.80
  108.8 1.4 collective-permute-start.2
  110.3 2.4 collective-permute-start.1
  112.7 1.4 collective-permute-start
  114.1 6.0 collective-permute-done.2
  120.2 9.9 %collective-permute-done.1 = bf16[128,1,2,512]{0,3,2,1:T(8,128)(2,1)S(1)} collective-permute-done((bf16[128,1,2,512]{0,3,2,1:T(8,128)(2,1)}, bf16[128,1,2,512]{0,3,2,1:T(8,128)(2,1)S(1)}, u32[]{:S(2)}, u32[]{:S(2)}) %collective-permute-start.1) | collective-permute-done | bytes 262176 | tf_op jit(solution)/shard_map/ppermute | solution.py:16
  130.1 2.3 fusion.66
  132.4 0.3 reduce-scatter.7.cloned.1.call-start
  132.6 57.8 %all-gather.5.cloned.1.call-done = bf16[512,1,2,4096]{0,3,2,1:T(8,128)(2,1)} async-done(((bf16[512,1,2,512]{0,3,2,1:T(8,128)(2,1)}), bf16[512,1,2,4096]{0,3,2,1:T(8,128)(2,1)}) %all-gather.5.cloned.1.call-update) | async-done | bytes 8388624 | tf_op jit(solution)/shard_map/all_gather | solution.py:59
  190.4 15.0 %fusion.4 = f32[512,2048]{1,0:T(8,128)} fusion(bf16[2,2048,4096]{2,1,0:T(8,128)(2,1)} %param.9, bf16[512,8192]{0,1:T(8,128)(2,1)} %bitcast.90), kind=kOutput, calls=%fused_computation.9 | convolution fusion | flops 8589934592 | bytes 25165824 | tf_op jit(solution)/shard_map/dot_general | solution.py:66
  205.4 15.0 %fusion.6 = f32[512,2048]{1,0:T(8,128)} fusion(bf16[2,2048,4096]{2,1,0:T(8,128)(2,1)} %param.9, bf16[512,8192]{0,1:T(8,128)(2,1)} %bitcast.91), kind=kOutput, calls=%fused_computation.11 | convolution fusion | flops 8589934592 | bytes 25165824 | tf_op jit(solution)/shard_map/dot_general | solution.py:66
  220.4 14.7 %add_convert_fusion.1 = bf16[512,2048]{1,0:T(8,128)(2,1)S(1)} fusion(f32[512,2048]{1,0:T(8,128)} %fusion.4, bf16[2,2048,4096]{2,1,0:T(8,128)(2,1)} %param.9, bf16[512,8192]{0,1:T(8,128)(2,1)} %bitcast.92), kind=kOutput, calls=%fused_computation.33 | convolution fusion | flops 8592031744 | bytes 27262976 | tf_op jit(solution)/shard_map/dot_general | solution.py:66
  235.2 14.3 %subtract_convert_fusion.1 = bf16[512,2048]{1,0:T(8,128)(2,1)S(1)} fusion(f32[512,2048]{1,0:T(8,128)} %fusion.6, bf16[2,2048,4096]{2,1,0:T(8,128)(2,1)} %param.9, bf16[512,8192]{0,1:T(8,128)(2,1)} %bitcast.93), kind=kOutput, calls=%fused_computation.34 | convolution fusion | flops 8592031744 | bytes 27262976 | tf_op jit(solution)/shard_map/dot_general | solution.py:66
  249.5 2.2 pad_maximum_fusion
  251.8 76.9 %reduce-scatter.7.cloned.1.call-done = bf16[128,4096]{1,0:T(8,128)(2,1)} async-done(((bf16[512,4096]{1,0:T(8,128)(2,1)}), bf16[128,4096]{1,0:T(8,128)(2,1)}) %reduce-scatter.7.cloned.1.call-update) | async-done | bytes 1048592 | tf_op jit(solution)/shard_map/reduce_scatter | solution.py:70
  328.7 1.8 reshape.159
  330.5 3.1 copy.31
  333.8 54.8 %all-gather.7.cloned.1.call-done = bf16[128,2,16384]{0,1,2:T(2,128)(2,1)} async-done(((bf16[128,2,2048]{0,1,2:T(2,128)(2,1)}), bf16[128,2,16384]{0,1,2:T(2,128)(2,1)}) %all-gather.7.cloned.1.call-update) | async-done | bytes 8388624 | tf_op jit(solution)/shard_map/all_gather | solution.py:77
  388.6 10.6 %gather_fusion.1 = bf16[2048,128,2]{1,2,0:T(2,128)(2,1)S(1)} fusion(bf16[128,2,16384]{0,1,2:T(2,128)(2,1)} %all-gather.7.cloned.1.call-done, s32[2048]{0:T(1024)S(1)} %broadcast_clamp_fusion), kind=kCustom, calls=%fused_computation.1 | custom fusion | bytes 2105344 | tf_op jit(solution)/shard_map/gather | solution.py:79
  399.1 0.8 convert_bitcast_fusion.1
  399.9 0.1 copy.32
  400.1 0.2 copy.33
  400.3 0.3 fusion.52
  400.7 0.4 copy-done.6
  401.1 0.7 convolution_convert_fusion.1
  401.9 15.8 %scatter_custom_fusion.1 = bf16[128,32768]{0,1:T(8,128)(2,1)} fusion(s32[4096]{0:T(1024)S(1)} %bitcast.89, bf16[4096,128]{1,0:T(8,128)(2,1)S(1)} %bitcast.82, bf16[]{:T(256)} %constant.73.clone.1), kind=kCustom, calls=%fused_computation.35 | custom fusion | bytes 8388610 | tf_op jit(solution)/shard_map/scatter | solution.py:53
  417.8 71.5 %reduce-scatter.9.cloned.1.call-done = bf16[128,4,2,512]{0,3,2,1:T(8,128)(2,1)} async-done(((bf16[128,4,2,4096]{0,3,2,1:T(8,128)(2,1)}), bf16[128,4,2,512]{0,3,2,1:T(8,128)(2,1)}) %reduce-scatter.9.cloned.1.call-update) | async-done | bytes 1048592 | tf_op jit(solution)/shard_map/reduce_scatter | solution.py:55
  489.3 1.6 fusion.62
  491.0 1.5 collective-permute-start.5
  492.5 2.4 collective-permute-start.4
  494.9 1.4 collective-permute-start.3
  496.3 5.8 collective-permute-done.5
  502.1 9.9 %collective-permute-done.4 = bf16[128,1,2,512]{0,3,2,1:T(8,128)(2,1)S(1)} collective-permute-done((bf16[128,1,2,512]{0,3,2,1:T(8,128)(2,1)S(1)}, bf16[128,1,2,512]{0,3,2,1:T(8,128)(2,1)S(1)}, u32[]{:S(2)}, u32[]{:S(2)}) %collective-permute-start.4) | collective-permute-done | bytes 262176 | tf_op jit(solution)/shard_map/ppermute | solution.py:16
  512.1 2.3 fusion.58
  514.4 58.0 %all-gather.9.cloned.1.call-done = bf16[512,1,2,4096]{0,3,2,1:T(8,128)(2,1)} async-done(((bf16[512,1,2,512]{0,3,2,1:T(8,128)(2,1)}), bf16[512,1,2,4096]{0,3,2,1:T(8,128)(2,1)}) %all-gather.9.cloned.1.call-update) | async-done | bytes 8388624 | tf_op jit(solution)/shard_map/all_gather | solution.py:59
  572.4 17.3 %fusion = f32[512,2048]{1,0:T(8,128)} fusion(bf16[2,2048,4096]{2,1,0:T(8,128)(2,1)} %param.9, bf16[512,8192]{0,1:T(8,128)(2,1)} %bitcast.94), kind=kOutput, calls=%fused_computation.5 | convolution fusion | flops 8589934592 | bytes 25165824 | tf_op jit(solution)/shard_map/dot_general | solution.py:66
  589.7 14.0 %fusion.2 = f32[512,2048]{1,0:T(8,128)} fusion(bf16[2,2048,4096]{2,1,0:T(8,128)(2,1)} %param.9, bf16[512,8192]{0,1:T(8,128)(2,1)S(1)} %bitcast.97), kind=kOutput, calls=%fused_computation.7 | convolution fusion | flops 8589934592 | bytes 25165824 | tf_op jit(solution)/shard_map/dot_general | solution.py:66
  603.7 14.6 %add_convert_fusion = bf16[512,2048]{1,0:T(8,128)(2,1)S(1)} fusion(f32[512,2048]{1,0:T(8,128)} %fusion, bf16[2,2048,4096]{2,1,0:T(8,128)(2,1)} %param.9, bf16[512,8192]{0,1:T(8,128)(2,1)} %bitcast.95), kind=kOutput, calls=%fused_computation.31 | convolution fusion | flops 8592031744 | bytes 27262976 | tf_op jit(solution)/shard_map/dot_general | solution.py:66
  618.3 14.3 %subtract_convert_fusion = bf16[512,2048]{1,0:T(8,128)(2,1)S(1)} fusion(f32[512,2048]{1,0:T(8,128)} %fusion.2, bf16[2,2048,4096]{2,1,0:T(8,128)(2,1)} %param.9, bf16[512,8192]{0,1:T(8,128)(2,1)} %bitcast.96), kind=kOutput, calls=%fused_computation.32 | convolution fusion | flops 8592031744 | bytes 27262976 | tf_op jit(solution)/shard_map/dot_general | solution.py:66
  632.6 2.2 pad_maximum_fusion.1
  634.9 76.9 %reduce-scatter.11.cloned.1.call-done = bf16[128,4096]{1,0:T(8,128)(2,1)} async-done(((bf16[512,4096]{1,0:T(8,128)(2,1)}), bf16[128,4096]{1,0:T(8,128)(2,1)}) %reduce-scatter.11.cloned.1.call-update) | async-done | bytes 1048592 | tf_op jit(solution)/shard_map/reduce_scatter | solution.py:70
  711.8 2.1 reshape.165
  713.9 3.1 copy.36
  717.0 54.9 %all-gather.11.cloned.1.call-done = bf16[128,2,16384]{0,1,2:T(2,128)(2,1)} async-done(((bf16[128,2,2048]{0,1,2:T(2,128)(2,1)}), bf16[128,2,16384]{0,1,2:T(2,128)(2,1)}) %all-gather.11.cloned.1.call-update) | async-done | bytes 8388624 | tf_op jit(solution)/shard_map/all_gather | solution.py:77
  771.9 10.4 %gather_fusion.2 = bf16[2048,128,2]{1,2,0:T(2,128)(2,1)S(1)} fusion(bf16[128,2,16384]{0,1,2:T(2,128)(2,1)} %all-gather.11.cloned.1.call-done, s32[2048]{0:T(1024)S(1)} %broadcast_clamp_fusion), kind=kCustom, calls=%fused_computation.2 | custom fusion | bytes 2105344 | tf_op jit(solution)/shard_map/gather | solution.py:79
  782.4 0.8 convert_bitcast_fusion
  783.2 0.1 copy.37
  783.3 0.2 copy.38
  783.6 0.3 fusion.53
  783.9 0.4 copy-done.3
  784.4 0.2 copy-done.5
  784.5 0.2 copy-done.7
  784.7 0.7 fusion.54
  785.4 1.7 copy.40
  (41 shorter events, 0.9 us)
Async XLA Ops:
  7.2 6.1 copy-start.1
  7.2 99.2 %reduce-scatter.5.cloned.1.call-start = ((), (), s32[]{:S(2)}) async-start(), calls=%async_computation.4 | async-start | bytes 9437184 | tf_op jit(solution)/shard_map/reduce_scatter | solution.py:55
  8.6 392.1 %copy-start.2 = (bf16[32,64,64]{1,2,0:T(8,128)(2,1)}, bf16[32,64,64]{1,2,0:T(8,128)(2,1)S(1)}, u32[]{:S(2)}) copy-start(bf16[32,64,64]{1,2,0:T(8,128)(2,1)S(1)} %fusion.77) | copy-start | bytes 786436
  11.0 389.7 %copy-start.4 = (bf16[32,64,64]{1,2,0:T(8,128)(2,1)}, bf16[32,64,64]{1,2,0:T(8,128)(2,1)S(1)}, u32[]{:S(2)}) copy-start(bf16[32,64,64]{1,2,0:T(8,128)(2,1)S(1)} %get-tuple-element.20) | copy-start | bytes 786436
  32.1 158.3 %all-gather.5.cloned.1.call-start = ((), (), s32[]{:S(2)}) async-start(), calls=%async_computation.5 | async-start | bytes 9437184 | tf_op jit(solution)/shard_map/all_gather | solution.py:59
  108.8 11.3 %collective-permute-start.2 = (bf16[128,1,2,512]{0,3,2,1:T(8,128)(2,1)}, bf16[128,1,2,512]{0,3,2,1:T(8,128)(2,1)S(1)}, u32[]{:S(2)}, u32[]{:S(2)}) collective-permute-start(bf16[128,1,2,512]{0,3,2,1:T(8,128)(2,1)} %get-tuple-element.17), channel_id=1, source_target_pairs={{0,1},{1,2},{2,3},{3,0},{4,5},{5,6},{6,7},{7,4},{8,9},{9,10},{10,1... | collective-permute-start | bytes 786440 | tf_op jit(solution)/shard_map/ppermute | solution.py:16
  110.3 19.8 %collective-permute-start.1 = (bf16[128,1,2,512]{0,3,2,1:T(8,128)(2,1)}, bf16[128,1,2,512]{0,3,2,1:T(8,128)(2,1)S(1)}, u32[]{:S(2)}, u32[]{:S(2)}) collective-permute-start(bf16[128,1,2,512]{0,3,2,1:T(8,128)(2,1)} %get-tuple-element.18), channel_id=1, source_target_pairs={{0,2},{1,3},{2,0},{3,1},{4,6},{5,7},{6,4},{7,5},{8,10},{9,11},{10,... | collective-permute-start | bytes 786440 | tf_op jit(solution)/shard_map/ppermute | solution.py:16
  112.7 17.4 %collective-permute-start = (bf16[128,1,2,512]{0,3,2,1:T(8,128)(2,1)S(1)}, bf16[128,1,2,512]{0,3,2,1:T(8,128)(2,1)S(1)}, u32[]{:S(2)}, u32[]{:S(2)}) collective-permute-start(bf16[128,1,2,512]{0,3,2,1:T(8,128)(2,1)S(1)} %get-tuple-element.19), channel_id=1, source_target_pairs={{0,3},{1,0},{2,1},{3,2},{4,7},{5,4},{6,5},{7,6},{8,11},{9,8},{10,9... | collective-permute-start | bytes 786440 | tf_op jit(solution)/shard_map/ppermute | solution.py:16
  132.4 196.3 %reduce-scatter.7.cloned.1.call-start = ((), (), s32[]{:S(2)}) async-start(), calls=%async_computation.6 | async-start | bytes 5242880 | tf_op jit(solution)/shard_map/reduce_scatter | solution.py:70
  251.8 136.8 %all-gather.7.cloned.1.call-start = ((), (), s32[]{:S(2)}) async-start(), calls=%async_computation.7 | async-start | bytes 9437184 | tf_op jit(solution)/shard_map/all_gather | solution.py:77
  333.6 155.7 %reduce-scatter.9.cloned.1.call-start = ((), (), s32[]{:S(2)}) async-start(), calls=%async_computation.8 | async-start | bytes 9437184 | tf_op jit(solution)/shard_map/reduce_scatter | solution.py:55
  400.1 1.0 copy-start.6
  417.7 154.7 %all-gather.9.cloned.1.call-start = ((), (), s32[]{:S(2)}) async-start(), calls=%async_computation.9 | async-start | bytes 9437184 | tf_op jit(solution)/shard_map/all_gather | solution.py:59
  491.0 11.2 %collective-permute-start.5 = (bf16[128,1,2,512]{0,3,2,1:T(8,128)(2,1)S(1)}, bf16[128,1,2,512]{0,3,2,1:T(8,128)(2,1)S(1)}, u32[]{:S(2)}, u32[]{:S(2)}) collective-permute-start(bf16[128,1,2,512]{0,3,2,1:T(8,128)(2,1)S(1)} %get-tuple-element.13), channel_id=1, source_target_pairs={{0,1},{1,2},{2,3},{3,0},{4,5},{5,6},{6,7},{7,4},{8,9},{9,10},{10,1... | collective-permute-start | bytes 786440 | tf_op jit(solution)/shard_map/ppermute | solution.py:16
  492.5 19.6 %collective-permute-start.4 = (bf16[128,1,2,512]{0,3,2,1:T(8,128)(2,1)S(1)}, bf16[128,1,2,512]{0,3,2,1:T(8,128)(2,1)S(1)}, u32[]{:S(2)}, u32[]{:S(2)}) collective-permute-start(bf16[128,1,2,512]{0,3,2,1:T(8,128)(2,1)S(1)} %get-tuple-element.14), channel_id=1, source_target_pairs={{0,2},{1,3},{2,0},{3,1},{4,6},{5,7},{6,4},{7,5},{8,10},{9,11},{10,... | collective-permute-start | bytes 786440 | tf_op jit(solution)/shard_map/ppermute | solution.py:16
  494.9 17.2 %collective-permute-start.3 = (bf16[128,1,2,512]{0,3,2,1:T(8,128)(2,1)S(1)}, bf16[128,1,2,512]{0,3,2,1:T(8,128)(2,1)S(1)}, u32[]{:S(2)}, u32[]{:S(2)}) collective-permute-start(bf16[128,1,2,512]{0,3,2,1:T(8,128)(2,1)S(1)} %get-tuple-element.15), channel_id=1, source_target_pairs={{0,3},{1,0},{2,1},{3,2},{4,7},{5,4},{6,5},{7,6},{8,11},{9,8},{10,9... | collective-permute-start | bytes 786440 | tf_op jit(solution)/shard_map/ppermute | solution.py:16
  514.4 197.5 %reduce-scatter.11.cloned.1.call-start = ((), (), s32[]{:S(2)}) async-start(), calls=%async_computation.10 | async-start | bytes 5242880 | tf_op jit(solution)/shard_map/reduce_scatter | solution.py:70
  572.4 17.3 %copy-start.8 = (bf16[512,1,2,4096]{0,3,2,1:T(8,128)(2,1)S(1)}, bf16[512,1,2,4096]{0,3,2,1:T(8,128)(2,1)}, u32[]{:S(2)}) copy-start(bf16[512,1,2,4096]{0,3,2,1:T(8,128)(2,1)} %all-gather.9.cloned.1.call-done) | copy-start | bytes 25165828
  634.9 137.1 %all-gather.11.cloned.1.call-start = ((), (), s32[]{:S(2)}) async-start(), calls=%async_computation.11 | async-start | bytes 9437184 | tf_op jit(solution)/shard_map/all_gather | solution.py:77
  713.9 69.2 %copy-start = (bf16[128,2,2048]{2,1,0:T(2,128)(2,1)}, bf16[128,2,2048]{2,1,0:T(2,128)(2,1)S(1)}, u32[]{:S(2)}) copy-start(bf16[128,2,2048]{2,1,0:T(2,128)(2,1)S(1)} %reshape.165) | copy-start | bytes 3145732
  783.3 1.0 copy-start.3
  783.3 1.2 copy-start.5
  783.3 1.3 copy-start.7
Sparse Core Ops, SparseCore 0:
  32.2 74.1 reduce-scatter.4
  132.5 57.8 all-gather.4
  251.9 76.7 reduce-scatter.6
  333.7 54.7 all-gather.6
  417.9 71.3 reduce-scatter.8
  514.5 57.8 all-gather.8
  635.0 76.7 reduce-scatter.10
  717.2 54.7 all-gather.10
